TPU v7x, 32 devices: a whole 2x2x4 slice. The times are simulated.
32 devices in a mesh: dp: 8 (over z, y), tensor: 4 (over x, core).
Axes of the slice: x: 2, y: 2, z: 4, core: 2. Of those that a mesh axis runs over, the one named last changes fastest.
Arguments:
- tokens: bfloat16 [16384, 1024], P(('dp', 'tensor')), may hold values from -6 to 6
- ln_gain: float32 [1024], replicated, may hold values from 0.1 to 1.9
- ln_bias: float32 [1024], replicated, may hold values from -1.75 to 1.75
- w_qkv: bfloat16 [3, 1024, 16, 64], P(None, None, 'tensor'), may hold values from -0.1875 to 0.1875
- b_qkv: float32 [3, 16, 64], P(None, 'tensor'), may hold values from -3 to 3
- w_in: bfloat16 [1024, 4096], P(None, 'tensor'), may hold values from -0.1875 to 0.1875
- b_in: float32 [4096], P('tensor'), may hold values from -3 to 3
- w_out: bfloat16 [16, 64, 1024], P('tensor'), may hold values from -1.5 to 1.5
- w_down: bfloat16 [4096, 1024], P('tensor'), may hold values from -0.09375 to 0.09375
- b_out: float32 [1024], replicated, may hold values from -3 to 3
- cotangent: bfloat16 [16384, 1024], P(('dp', 'tensor')), may hold values from -6 to 6
- block_doc: int32 [8, 4], P('dp'), may hold values from 0 to 2, as said below
Outputs:
- block_out: bfloat16 [16384, 1024], P(('dp', 'tensor'))
- grad_tokens: float32 [16384, 1024], P(('dp', 'tensor'))
- grad_ln_gain: float32 [1024], replicated
- grad_ln_bias: float32 [1024], replicated
- grad_w_qkv: float32 [3, 1024, 16, 64], P(None, 'dp', 'tensor')
- grad_b_qkv: float32 [3, 16, 64], replicated
- grad_w_in: float32 [1024, 4096], P('dp', 'tensor')
- grad_b_in: float32 [4096], replicated
- grad_w_out: float32 [16, 64, 1024], P('tensor', None, 'dp')
- grad_w_down: float32 [4096, 1024], P('tensor', 'dp')
- grad_b_out: float32 [1024], replicated
Inputs may be any that keep to these rules, and one draw needn't show every extreme that they name: `block_doc`: in each group the numbers start at 0 and rise by 0 or 1 from block to block. Every sequence covers a power of two of blocks, at most 2; a sequence of k blocks starts at a block index divisible by k; each group has a sequence of exactly 2 blocks.
All inputs are finite; a program needn't handle non-finite values.
Results may differ from a plain program's by a relative error of at most 0.012.
The roundings to bfloat16 on the way count: a program that leaves them out, or rounds other values in their place, can miss the bound.
Values may be sent and summed in bfloat16 or wider, within the bound.
No kernel may reach another device: no remote copies, remote signals or barrier semaphores. Data moves between devices by JAX's collectives and lax.ppermute only.
A program may use at most 256 MiB of HBM per device.

v0:
```python
from functools import partial
import jax
import jax.numpy as jnp
from jax import lax
from jax.sharding import PartitionSpec as P

HEADS = 16
FF = 4096
ROT = 16
BLK = 512
epsilon = 1e-05


def layer_norm(rows, ln_gain, ln_bias):
    mean_row = jnp.mean(rows, axis=-1, keepdims=True)
    centred = rows - mean_row
    var_row = jnp.mean(centred * centred, axis=-1, keepdims=True)
    return centred * lax.rsqrt(var_row + epsilon) * ln_gain + ln_bias


def rope_tables(positions):
    half_dims = ROT // 2
    inverse = 1.0 / 10000.0 ** (jnp.arange(half_dims, dtype=jnp.float32) * 2.0 / ROT)
    angles = positions[:, None] * inverse[None, :]
    return (jnp.cos(angles), jnp.sin(angles))


def rotate(vectors, cosine_table, sine_table):
    half_dims = ROT // 2
    leading = vectors[..., :half_dims]
    trailing = vectors[..., half_dims:ROT]
    remain = vectors[..., ROT:]
    cosine = cosine_table[:, None, :]
    sine = sine_table[:, None, :]
    return jnp.concatenate(
        [leading * cosine - trailing * sine, trailing * cosine + leading * sine, remain], axis=-1
    )


def shards(
    tokens, ln_gain, ln_bias, w_qkv, b_qkv, w_in, b_in, w_out, w_down, b_out, cotangent, block_doc
):
    rows_local = tokens.shape[0]
    model_width = tokens.shape[1]
    heads_local = w_qkv.shape[2]
    head_dim = w_qkv.shape[3]
    attn_cols = heads_local * head_dim
    hidden_local = w_in.shape[1]
    score_scale = head_dim ** (-0.5)
    token_values = tokens.astype(jnp.float32)
    normed_rows, ln_back = jax.vjp(layer_norm, token_values, ln_gain, ln_bias)
    normed_low = normed_rows.astype(jnp.bfloat16)
    gathered = lax.all_gather(normed_low, "tensor", axis=0, tiled=True)
    group_rows = gathered.shape[0]
    num_blocks = group_rows // BLK
    seq_blocks = min(4, num_blocks // 2)
    window = seq_blocks * BLK
    pad_rows = window - BLK
    joined_weight = jnp.concatenate(
        [
            w_qkv[0].reshape(model_width, attn_cols),
            w_qkv[1].reshape(model_width, attn_cols),
            w_qkv[2].reshape(model_width, attn_cols),
            w_in,
        ],
        axis=1,
    )
    joined_bias = jnp.concatenate([b_qkv.reshape(3 * attn_cols), b_in])
    upward = jnp.dot(gathered, joined_weight, preferred_element_type=jnp.float32) + joined_bias
    query_pre = upward[:, :attn_cols].reshape(group_rows, heads_local, head_dim)
    key_pre = upward[:, attn_cols : 2 * attn_cols].reshape(group_rows, heads_local, head_dim)
    value_pre = upward[:, 2 * attn_cols : 3 * attn_cols].reshape(group_rows, heads_local, head_dim)
    hidden_pre = upward[:, 3 * attn_cols :]
    sequence_ids = block_doc[0]
    block_starts = jnp.sum(
        (sequence_ids[None, :] < sequence_ids[:, None]).astype(jnp.int32), axis=1
    )
    positions = (
        jnp.arange(group_rows, dtype=jnp.int32) - jnp.repeat(block_starts, BLK) * BLK
    ).astype(jnp.float32)
    cosine_table, sine_table = rope_tables(positions)
    all_queries = rotate(query_pre, cosine_table, sine_table).astype(jnp.bfloat16)
    all_keys = rotate(key_pre, cosine_table, sine_table).astype(jnp.bfloat16)
    all_values = value_pre.astype(jnp.bfloat16)
    pad_heads = jnp.zeros((pad_rows, heads_local, head_dim), jnp.bfloat16)
    keys_padded = jnp.concatenate([pad_heads, all_keys], axis=0)
    values_padded = jnp.concatenate([pad_heads, all_values], axis=0)
    padded_docs = jnp.concatenate([jnp.full((seq_blocks - 1,), -1, jnp.int32), sequence_ids])
    key_docs = jnp.repeat(padded_docs, BLK)
    query_offset = lax.broadcasted_iota(jnp.int32, (BLK, window), 0)
    key_offset = lax.broadcasted_iota(jnp.int32, (BLK, window), 1)
    causal = key_offset - pad_rows <= query_offset

    def window_scores(query_block):
        first_row = query_block * BLK
        query_rows = lax.dynamic_slice_in_dim(all_queries, first_row, BLK, 0)
        key_rows = lax.dynamic_slice_in_dim(keys_padded, first_row, window, 0)
        value_rows = lax.dynamic_slice_in_dim(values_padded, first_row, window, 0)
        window_docs = lax.dynamic_slice_in_dim(key_docs, first_row, window, 0)
        allowed = (window_docs[None, :] == sequence_ids[query_block]) & causal
        scores = (
            jnp.einsum("qhe,khe->hqk", query_rows, key_rows, preferred_element_type=jnp.float32)
            * score_scale
        )
        return (query_rows, key_rows, value_rows, jnp.where(allowed[None], scores, -1e30))

    def attend(query_block):
        query_rows, key_rows, value_rows, scores = window_scores(query_block)
        maxima = jnp.max(scores, axis=-1)
        log_total = maxima + jnp.log(jnp.sum(jnp.exp(scores - maxima[..., None]), axis=-1))
        weights = jax.nn.softmax(scores, axis=-1).astype(jnp.bfloat16)
        out_rows = jnp.einsum(
            "hqk,khe->qhe", weights, value_rows, preferred_element_type=jnp.float32
        )
        return (out_rows, log_total)

    attended_blocks, log_totals = lax.map(attend, jnp.arange(num_blocks, dtype=jnp.int32))
    attended = attended_blocks.reshape(group_rows, attn_cols).astype(jnp.bfloat16)
    w_out_flat = w_out.reshape(attn_cols, model_width)
    active_full, gelu_back = jax.vjp(partial(jax.nn.gelu, approximate=False), hidden_pre)
    active = active_full.astype(jnp.bfloat16)
    active_rows = lax.dynamic_slice_in_dim(
        active, jnp.int32(0), rows_local * lax.axis_size("tensor"), 0
    )
    mixed = lax.psum_scatter(
        jnp.dot(attended, w_out_flat, preferred_element_type=jnp.float32)
        + jnp.dot(active_rows, w_down, preferred_element_type=jnp.float32),
        "tensor",
        scatter_dimension=0,
        tiled=True,
    )
    block_out = (token_values + mixed + b_out).astype(jnp.bfloat16)
    cotangent_group = lax.all_gather(cotangent, "tensor", axis=0, tiled=True)
    grad_attended = jnp.einsum(
        "td,cd->tc", cotangent_group, w_out_flat, preferred_element_type=jnp.float32
    ).astype(jnp.bfloat16)
    grad_active = jnp.einsum(
        "td,fd->tf", cotangent_group, w_down, preferred_element_type=jnp.float32
    )
    grad_w_out = jnp.einsum(
        "tc,td->cd", attended, cotangent_group, preferred_element_type=jnp.float32
    )
    grad_w_down = jnp.einsum(
        "tf,td->fd", active, cotangent_group, preferred_element_type=jnp.float32
    )
    grad_hidden = gelu_back(grad_active)[0].astype(jnp.bfloat16)
    grad_out_heads = grad_attended.reshape(group_rows, heads_local, head_dim)

    def back_block(query_block, carried):
        grad_q_all, grad_k_padded, grad_v_padded = carried
        first_row = query_block * BLK
        query_rows, key_rows, value_rows, scores = window_scores(query_block)
        grad_rows_out = lax.dynamic_slice_in_dim(grad_out_heads, first_row, BLK, 0)
        weights = jnp.exp(scores - log_totals[query_block][..., None])
        grad_weights = jnp.einsum(
            "qhe,khe->hqk", grad_rows_out, value_rows, preferred_element_type=jnp.float32
        )
        deltas = jnp.sum(weights * grad_weights, axis=-1)
        grad_scores = (weights * (grad_weights - deltas[..., None])).astype(jnp.bfloat16)
        grad_q_rows = (
            jnp.einsum("hqk,khe->qhe", grad_scores, key_rows, preferred_element_type=jnp.float32)
            * score_scale
        )
        grad_k_rows = (
            jnp.einsum("hqk,qhe->khe", grad_scores, query_rows, preferred_element_type=jnp.float32)
            * score_scale
        )
        grad_v_rows = jnp.einsum(
            "hqk,qhe->khe",
            weights.astype(jnp.bfloat16),
            grad_rows_out,
            preferred_element_type=jnp.float32,
        )
        old_k = lax.dynamic_slice_in_dim(grad_k_padded, first_row, window, 0)
        old_v = lax.dynamic_slice_in_dim(grad_v_padded, first_row, window, 0)
        grad_k_padded = lax.dynamic_update_slice_in_dim(
            grad_k_padded, old_k + grad_k_rows, first_row, 0
        )
        grad_v_padded = lax.dynamic_update_slice_in_dim(
            grad_v_padded, old_v + grad_v_rows, first_row, 0
        )
        grad_q_all = lax.dynamic_update_slice_in_dim(grad_q_all, grad_q_rows, first_row, 0)
        return (grad_q_all, grad_k_padded, grad_v_padded)

    zero_heads = jnp.zeros((group_rows, heads_local, head_dim), jnp.float32)
    zero_padded = jnp.zeros((group_rows + pad_rows, heads_local, head_dim), jnp.float32)
    grad_queries, grad_k_padded, grad_v_padded = lax.fori_loop(
        0, num_blocks, back_block, (zero_heads, zero_padded, zero_padded)
    )
    grad_keys = grad_k_padded[pad_rows:]
    grad_values = grad_v_padded[pad_rows:]
    grad_q_pre = (
        rotate(grad_queries, cosine_table, -sine_table)
        .astype(jnp.bfloat16)
        .reshape(group_rows, attn_cols)
    )
    grad_k_pre = (
        rotate(grad_keys, cosine_table, -sine_table)
        .astype(jnp.bfloat16)
        .reshape(group_rows, attn_cols)
    )
    grad_v_pre = grad_values.astype(jnp.bfloat16).reshape(group_rows, attn_cols)
    grad_upward = jnp.concatenate([grad_q_pre, grad_k_pre, grad_v_pre, grad_hidden], axis=1)
    grad_joined_weight = jnp.einsum(
        "td,tc->dc", gathered, grad_upward, preferred_element_type=jnp.float32
    )
    grad_joined_bias = jnp.sum(grad_upward, axis=0, dtype=jnp.float32)
    grad_normed = lax.psum_scatter(
        jnp.einsum("tc,dc->td", grad_upward, joined_weight, preferred_element_type=jnp.float32),
        "tensor",
        scatter_dimension=0,
        tiled=True,
    )
    grad_tokens_norm, grad_gain_part, grad_bias_part = ln_back(grad_normed)
    grad_tokens = grad_tokens_norm + cotangent.astype(jnp.float32)
    grad_bout_part = jnp.sum(cotangent, axis=0, dtype=jnp.float32)
    grad_w_qkv_local = jnp.stack(
        [
            grad_joined_weight[:, member * attn_cols : (member + 1) * attn_cols].reshape(
                model_width, heads_local, head_dim
            )
            for member in range(3)
        ]
    )
    grad_w_in_local = grad_joined_weight[:, 3 * attn_cols :]
    tensor_rank = lax.axis_index("tensor")
    bqkv_full = lax.dynamic_update_slice(
        jnp.zeros((3, HEADS, head_dim), jnp.float32),
        grad_joined_bias[: 3 * attn_cols].reshape(3, heads_local, head_dim),
        (jnp.int32(0), tensor_rank * heads_local, jnp.int32(0)),
    )
    bin_full = lax.dynamic_update_slice(
        jnp.zeros((FF,), jnp.float32),
        grad_joined_bias[3 * attn_cols :],
        (tensor_rank * hidden_local,),
    )
    grad_ln_gain, grad_ln_bias, grad_b_out, grad_b_qkv, grad_b_in = lax.psum(
        (grad_gain_part, grad_bias_part, grad_bout_part, bqkv_full, bin_full), ("dp", "tensor")
    )
    grad_w_qkv, grad_w_in, grad_w_out_part, grad_w_down_part = (
        lax.psum_scatter(grad_w_qkv_local, "dp", scatter_dimension=1, tiled=True),
        lax.psum_scatter(grad_w_in_local, "dp", scatter_dimension=0, tiled=True),
        lax.psum_scatter(
            grad_w_out.reshape(heads_local, head_dim, model_width),
            "dp",
            scatter_dimension=2,
            tiled=True,
        ),
        lax.psum_scatter(grad_w_down, "dp", scatter_dimension=1, tiled=True),
    )
    return (
        block_out,
        grad_tokens,
        grad_ln_gain,
        grad_ln_bias,
        grad_w_qkv,
        grad_b_qkv,
        grad_w_in,
        grad_b_in,
        grad_w_out_part,
        grad_w_down_part,
        grad_b_out,
    )


def solution(mesh):
    return jax.shard_map(
        shards,
        mesh=mesh,
        in_specs=(
            P(("dp", "tensor"), None),
            P(),
            P(),
            P(None, None, "tensor", None),
            P(None, "tensor", None),
            P(None, "tensor"),
            P("tensor"),
            P("tensor", None, None),
            P("tensor", None),
            P(),
            P(("dp", "tensor"), None),
            P("dp", None),
        ),
        out_specs=(
            P(("dp", "tensor"), None),
            P(("dp", "tensor"), None),
            P(),
            P(),
            P(None, "dp", "tensor", None),
            P(),
            P("dp", "tensor"),
            P(),
            P("tensor", None, "dp"),
            P("tensor", "dp"),
            P(),
        ),
        check_vma=False,
    )
```

profile of v0, /device:TPU:0, one launch (start us, length us, event | category | flops | bytes accessed | tf_op | source)
XLA Modules:
  0.0 755.2 jit_solution(2105448763767745747)
XLA Ops:
  22.3 29.4 %all-gather.3.cloned.1.call-done = bf16[2048,1024]{1,0:T(8,128)(2,1)} async-done(((bf16[512,1024]{1,0:T(8,128)(2,1)}), bf16[2048,1024]{1,0:T(8,128)(2,1)}) %all-gather.3.cloned.1.call-update) | async-done | bytes 4194320 | tf_op jit(solution)/shard_map/all_gather | solution.py:53
  51.7 14.2 %convolution_add_fusion = f32[2048,1792]{0,1:T(8,128)} fusion(bf16[2048,1024]{1,0:T(8,128)(2,1)} %all-gather.3.cloned.1.call-done, f32[1792]{0:T(1024)S(1)} %pad_maximum_fusion.8, bf16[1024,1024]{1,0:T(8,128)(2,1)} %param.21, bf16[1024,256]{1,0:T(8,128)(2,1)S(1)} %copy.38, bf16[1024,256]{1,0:T(8,128)(2,1)} %copy.37, bf16[1024,256]{1,0:T(8,128)(2,1)} %copy.36), kind=kOutput, calls=%fused_computation.77 | convolution fusion | flops 7534542848 | bytes 22551552 | tf_op jit(solution)/shard_map/dot_general | solution.py:69
  74.0 59.7 %while.31 = (s32[]{:T(128)}, bf16[4,512,4,64]{1,3,2,0:T(8,128)(2,1)}, f32[4,4,512]{2,1,0:T(4,128)}, s32[4]{0:T(128)S(1)}, bf16[2560,4,64]{0,2,1:T(8,128)(2,1)}, ...) while((s32[]{:T(128)}, ...), condition=%wide.region_6.7_spmd.clone, body=%wide.region_3.6_spmd.clone.sunk | while | flops 563084288 | bytes 29175080 | solution.py:117
  133.8 4.7 convolution_convert_fusion
  143.6 80.2 %while.32 = (s32[]{:T(128)}, f32[2048,4,64]{0,2,1:T(8,128)}, f32[2560,4,64]{0,2,1:T(8,128)}, f32[2560,4,64]{0,2,1:T(8,128)}, bf16[2560,4,64]{0,2,1:T(8,128)(2,1)...) while((s32[]{:T(128)}, f32[2048,4,64]{0,2,1:T(8,128)}, ...), condition=%wide.region_10.11_spmd.clone, body=%wide.region_8.10_spmd.clone.sunk | while | flops 1375599616 | bytes 97585616 | solution.py:187
  159.4 4.5 fusion.143
  179.4 4.5 fusion.143
  199.3 4.5 fusion.143
  219.3 4.5 fusion.143
  230.4 26.7 %add_convert_fusion = (bf16[2048,1024]{0,1:T(8,128)(2,1)S(1)}, f32[2048,1024]{0,1:T(8,128)}) fusion(f32[2048,1792]{0,1:T(8,128)} %convolution_add_fusion, bf16[2048,1024]{1,0:T(8,128)(2,1)S(1)} %copy-done.29, bf16[1024,1024]{1,0:T(8,128)(2,1)S(1)} %copy-done), kind=kOutput, calls=%fused_computation.61 | convolution fusion | flops 4445962240 | bytes 27262976 | tf_op jit(solution)/shard_map/td,fd->tf/dot_general | solution.py:137
  259.2 12.7 %fusion.79 = f32[2048,1024]{1,0:T(8,128)} fusion(bf16[1024,1024]{1,0:T(8,128)(2,1)} %param.21, bf16[1024,256]{1,0:T(8,128)(2,1)S(1)} %copy-done.17, bf16[1024,256]{1,0:T(8,128)(2,1)S(1)} %copy-done.15, bf16[1024,256]{1,0:T(8,128)(2,1)S(1)} %copy-done.14, bf16[2048,1024]{0,1:T(8,128)(2,1)S(1)} %get-tuple-element.373, bf16[2048,256]{0,1:T(8,128)(2,1)S(1)} %bitcast.104, ...), kind=kOutput, calls=%fused_computation.119 | convolution fusion | flops 7560232960 | bytes 19398656 | tf_op jit(solution)/shard_map/tc,dc->td/dot_general | solution.py:209
  274.4 11.8 %multiply_convert_fusion.1 = bf16[2048,1024]{0,1:T(8,128)(2,1)} fusion(f32[2048,1024]{0,1:T(8,128)} %get-tuple-element.374, f32[2048,1792]{0,1:T(8,128)} %convolution_add_fusion), kind=kLoop, calls=%fused_computation.62 | loop fusion | flops 6291456 | bytes 20971520 | tf_op jit(solution)/shard_map/convert_element_type | solution.py:121
  286.2 6.6 fusion.91
  292.8 4.8 convolution_add_fusion.1
  302.4 12.4 %fusion.85 = f32[1024,1792]{1,0:T(8,128)S(1)} fusion(bf16[2048,1024]{1,0:T(8,128)(2,1)} %all-gather.3.cloned.1.call-done, bf16[2048,1024]{0,1:T(8,128)(2,1)} %copy-done.6, bf16[2048,256]{0,1:T(8,128)(2,1)} %bitcast.105, bf16[2048,256]{0,1:T(8,128)(2,1)} %bitcast.114, bf16[2048,256]{0,1:T(8,128)(2,1)} %bitcast.111), kind=kOutput, calls=%fused_computation.149 | convolution fusion | flops 7545552896 | bytes 18874368 | tf_op jit(solution)/shard_map/td,tc->dc/dot_general | solution.py:204
  330.0 4.8 slice.139
  335.1 10.1 %fusion.92 = f32[1024,1024]{1,0:T(8,128)} fusion(bf16[2048,1024]{0,1:T(8,128)(2,1)} %multiply_convert_fusion.1, bf16[2048,1024]{1,0:T(8,128)(2,1)} %all-gather.5.cloned.1.call-done), kind=kOutput, calls=%fused_computation.155 | convolution fusion | flops 4294967296 | bytes 12582912 | tf_op jit(solution)/shard_map/tf,td->fd/dot_general | solution.py:143
  354.4 63.1 %reduce-scatter.7.cloned.1.call-done = f32[512,1024]{1,0:T(8,128)} async-done(((f32[2048,1024]{1,0:T(8,128)}), f32[512,1024]{1,0:T(8,128)}) %reduce-scatter.7.cloned.1.call-update) | async-done | bytes 2097168 | tf_op jit(solution)/shard_map/reduce_scatter | solution.py:125
  417.5 5.1 convert_reduce_fusion.2
  422.7 40.9 %all-reduce.2 = (f32[1024]{0:T(1024)}, f32[1024]{0:T(1024)}, f32[3,16,64]{2,1,0:T(8,128)}, f32[4096]{0:T(1024)}, f32[1024]{0:T(1024)}) all-reduce(f32[1024]{0:T(1024)S(1)} %get-tuple-element.320, f32[1024]{0:T(1024)S(1)} %get-tuple-element.322, ...), channel_id=1, replica_groups=mesh['dp'=8,'tensor'=4] {'dp','tensor'}, use_global_device_ids=true, to_apply=%region_15.16 | all-reduce | flops 10240 | bytes 81920 | tf_op jit(solution)/shard_map/psum | solution.py:237
  463.6 22.5 %reduce-scatter.15.cloned.1.call-done = f32[4,64,128]{2,1,0:T(8,128)} async-done(((f32[4,64,1024]{2,1,0:T(8,128)}), f32[4,64,128]{2,1,0:T(8,128)}) %reduce-scatter.15.cloned.1.call-update) | async-done | bytes 131088 | tf_op jit(solution)/shard_map/reduce_scatter | solution.py:243
  486.1 77.8 %reduce-scatter.11.cloned.1.call-done = f32[3,128,4,64]{1,3,2,0:T(8,128)} async-done(((f32[3,1024,4,64]{1,3,2,0:T(8,128)}), f32[3,128,4,64]{1,3,2,0:T(8,128)}) %reduce-scatter.11.cloned.1.call-update) | async-done | bytes 393232 | tf_op jit(solution)/shard_map/reduce_scatter | solution.py:241
  563.8 91.7 %reduce-scatter.13.cloned.1.call-done = f32[128,1024]{1,0:T(8,128)} async-done(((f32[1024,1024]{1,0:T(8,128)}), f32[128,1024]{1,0:T(8,128)}) %reduce-scatter.13.cloned.1.call-update) | async-done | bytes 524304 | tf_op jit(solution)/shard_map/reduce_scatter | solution.py:242
  655.5 92.6 %reduce-scatter.17.cloned.1.call-done = f32[1024,128]{1,0:T(8,128)} async-done(((f32[1024,1024]{1,0:T(8,128)}), f32[1024,128]{1,0:T(8,128)}) %reduce-scatter.17.cloned.1.call-update) | async-done | bytes 524304 | tf_op jit(solution)/shard_map/reduce_scatter | solution.py:249
  (234 shorter events, 179.8 us)
Async XLA Ops:
  7.2 223.1 %copy-start = (bf16[1024,1024]{1,0:T(8,128)(2,1)S(1)}, bf16[1024,1024]{1,0:T(8,128)(2,1)}, u32[]{:S(2)}) copy-start(bf16[1024,1024]{1,0:T(8,128)(2,1)} %param.24) | copy-start | bytes 6291460
  7.2 13.6 %copy-start.26 = (f32[3,4,64]{2,1,0:T(4,128)S(1)}, f32[3,4,64]{2,1,0:T(4,128)}, u32[]{:S(2)}) copy-start(f32[3,4,64]{2,1,0:T(4,128)} %param.20) | copy-start | bytes 9220
  7.2 13.7 %copy-start.30 = (s32[1,4]{1,0:T(1,128)S(1)}, s32[1,4]{1,0:T(1,128)}, u32[]{:S(2)}) copy-start(s32[1,4]{1,0:T(1,128)} %param.27) | copy-start | bytes 52
  7.2 14.1 %copy-start.28 = (f32[1024]{0:T(1024)S(1)}, f32[1024]{0:T(1024)}, u32[]{:S(2)}) copy-start(f32[1024]{0:T(1024)} %param.22) | copy-start | bytes 12292
  7.2 44.5 %all-gather.3.cloned.1.call-start = ((), (), s32[]{:S(2)}) async-start(), calls=%async_computation.6 | async-start | bytes 5242880 | tf_op jit(solution)/shard_map/all_gather | solution.py:53
  14.4 119.4 %all-gather.5.cloned.1.call-start = ((), (), s32[]{:S(2)}) async-start(), calls=%async_computation.8 | async-start | bytes 5242880 | tf_op jit(solution)/shard_map/all_gather | solution.py:133
  15.1 334.6 %reduce-scatter.9.cloned.1.call-start = ((), (), s32[]{:S(2)}) async-start(), calls=%async_computation.9 | async-start | bytes 10485760 | tf_op jit(solution)/shard_map/reduce_scatter | solution.py:208
  20.8 45.1 %copy-start.16 = (bf16[1024,256]{1,0:T(8,128)(2,1)}, bf16[1024,256]{1,0:T(8,128)(2,1)S(1)}, u32[]{:S(2)}) copy-start(bf16[1024,256]{1,0:T(8,128)(2,1)S(1)} %copy.38) | copy-start | bytes 1572868
  22.3 48.1 %copy-start.11 = (f32[2048,8]{0,1:T(8,128)}, f32[2048,8]{0,1:T(8,128)S(1)}, u32[]{:S(2)}) copy-start(f32[2048,8]{0,1:T(8,128)S(1)} %get-tuple-element.404) | copy-start | bytes 196612
  133.8 9.9 %copy-start.1 = (bf16[2560,4,64]{0,2,1:T(8,128)(2,1)S(1)}, bf16[2560,4,64]{0,2,1:T(8,128)(2,1)}, u32[]{:S(2)}) copy-start(bf16[2560,4,64]{0,2,1:T(8,128)(2,1)} %get-tuple-element.658) | copy-start | bytes 3932164
  143.6 83.4 %copy-start.12 = (f32[2048,8]{0,1:T(8,128)S(1)}, f32[2048,8]{0,1:T(8,128)}, u32[]{:S(2)}) copy-start(f32[2048,8]{0,1:T(8,128)} %copy-done.11) | copy-start | bytes 196612
  143.6 83.4 %copy-start.18 = (f32[2048,8]{0,1:T(8,128)S(1)}, f32[2048,8]{0,1:T(8,128)}, u32[]{:S(2)}) copy-start(f32[2048,8]{0,1:T(8,128)} %get-tuple-element.402) | copy-start | bytes 196612
  230.2 27.0 %copy-start.7 = (bf16[2048,4,64]{0,2,1:T(8,128)(2,1)}, bf16[2048,4,64]{0,2,1:T(8,128)(2,1)S(1)}, u32[]{:S(2)}) copy-start(bf16[2048,4,64]{0,2,1:T(8,128)(2,1)S(1)} %slice.174) | copy-start | bytes 3145732
  230.3 26.8 %copy-start.8 = (bf16[2048,4,64]{0,2,1:T(8,128)(2,1)}, bf16[2048,4,64]{0,2,1:T(8,128)(2,1)S(1)}, u32[]{:S(2)}) copy-start(bf16[2048,4,64]{0,2,1:T(8,128)(2,1)S(1)} %get-tuple-element.405) | copy-start | bytes 3145732
  230.4 26.8 %copy-start.9 = (bf16[2048,4,64]{0,2,1:T(8,128)(2,1)}, bf16[2048,4,64]{0,2,1:T(8,128)(2,1)S(1)}, u32[]{:S(2)}) copy-start(bf16[2048,4,64]{0,2,1:T(8,128)(2,1)S(1)} %get-tuple-element.406) | copy-start | bytes 3145732
  230.4 28.8 %copy-start.14 = (bf16[1024,256]{1,0:T(8,128)(2,1)S(1)}, bf16[1024,256]{1,0:T(8,128)(2,1)}, u32[]{:S(2)}) copy-start(bf16[1024,256]{1,0:T(8,128)(2,1)} %copy.36) | copy-start | bytes 1572868
  230.4 28.8 %copy-start.15 = (bf16[1024,256]{1,0:T(8,128)(2,1)S(1)}, bf16[1024,256]{1,0:T(8,128)(2,1)}, u32[]{:S(2)}) copy-start(bf16[1024,256]{1,0:T(8,128)(2,1)} %copy.37) | copy-start | bytes 1572868
  230.4 28.8 %copy-start.17 = (bf16[1024,256]{1,0:T(8,128)(2,1)S(1)}, bf16[1024,256]{1,0:T(8,128)(2,1)}, u32[]{:S(2)}) copy-start(bf16[1024,256]{1,0:T(8,128)(2,1)} %copy-done.16) | copy-start | bytes 1572868
  271.9 145.6 %reduce-scatter.7.cloned.1.call-start = ((), (), s32[]{:S(2)}) async-start(), calls=%async_computation.7 | async-start | bytes 10485760 | tf_op jit(solution)/shard_map/reduce_scatter | solution.py:125
  297.6 188.5 %reduce-scatter.15.cloned.1.call-start = ((), (), s32[]{:S(2)}) async-start(), calls=%async_computation.12 | async-start | bytes 1179648 | tf_op jit(solution)/shard_map/reduce_scatter | solution.py:243
  302.1 261.7 %reduce-scatter.11.cloned.1.call-start = ((), (), s32[]{:S(2)}) async-start(), calls=%async_computation.10 | async-start | bytes 3538944 | tf_op jit(solution)/shard_map/reduce_scatter | solution.py:241
  329.9 325.6 %reduce-scatter.13.cloned.1.call-start = ((), (), s32[]{:S(2)}) async-start(), calls=%async_computation.11 | async-start | bytes 4718592 | tf_op jit(solution)/shard_map/reduce_scatter | solution.py:242
  334.8 413.3 %reduce-scatter.17.cloned.1.call-start = ((), (), s32[]{:S(2)}) async-start(), calls=%async_computation.13 | async-start | bytes 4718592 | tf_op jit(solution)/shard_map/reduce_scatter | solution.py:249
  345.2 72.3 %copy-start.27 = (f32[1024]{0:T(1024)S(1)}, f32[1024]{0:T(1024)}, u32[]{:S(2)}) copy-start(f32[1024]{0:T(1024)} %param.25) | copy-start | bytes 12292
  (28 other events, 95.1 us)
Sparse Core Ops, SparseCore 0:
  14.5 37.1 all-gather.2
  53.3 34.5 all-gather.4
  272.0 71.5 reduce-scatter.8
  346.1 71.4 reduce-scatter.6
  421.3 64.6 reduce-scatter.14
  490.1 73.6 reduce-scatter.10
  568.0 87.4 reduce-scatter.12
  659.7 88.3 reduce-scatter.16
where the time goes:
time: 760 us; the launch traced here: 755 us
  waiting for transfers between devices  378 us (50%)
  matrix products  185 us (24%)
  other arithmetic  70.6 us (9%)
  local copies, waits for them, and re-layouts  53.6 us (7%)
  blocking collectives  40.9 us (5%)
  between operations  14.9 us (2%)
  loops' own time  10.9 us (1%)
    reduce_scatter x1, waiting for transfers between devices, shards(): lax.psum_scatter(grad_w_down, 'dp', scatter_dimension=1, tiled=True)  92.6 us
    reduce_scatter x1, waiting for transfers between devices, shards(): lax.psum_scatter(grad_w_in_local, 'dp', scatter_dimension=0, tiled=True)  91.7 us
    reduce_scatter x1, waiting for transfers between devices, shards(): lax.psum_scatter(grad_w_qkv_local, 'dp', scatter_dimension=1, tiled=True)  77.8 us
    reduce_scatter x1, waiting for transfers between devices, shards(): lax.psum_scatter(jnp.dot(attended, w_out_flat, preferred_element_type=jnp...  63.1 us
    psum x1, blocking collectives, shards(): lax.psum((grad_gain_part, grad_bias_part, grad_bout_part, bqkv_full, bin_...  40.9 us
    all_gather x1, waiting for transfers between devices, shards(): gathered = lax.all_gather(normed_low, 'tensor', axis=0, tiled=True)  29.4 us
    dot_general x1, matrix products, shards(): jnp.einsum('td,fd->tf', cotangent_group, w_down, preferred_element_type=j...  26.7 us
    reduce_scatter x1, waiting for transfers between devices, shards(): lax.psum_scatter(grad_w_out.reshape(heads_local, head_dim, model_width),...  22.5 us
  transfers between devices with their start and end apart: 8, of which 6 were waited for; matrix products, arithmetic and copies ran while one was open for 21% of the time, Pallas kernels for 0%

commit v1 on v0

--- a/solution.py
+++ b/solution.py
@@ -50,7 +50,24 @@
     token_values = tokens.astype(jnp.float32)
     normed_rows, ln_back = jax.vjp(layer_norm, token_values, ln_gain, ln_bias)
     normed_low = normed_rows.astype(jnp.bfloat16)
-    gathered = lax.all_gather(normed_low, "tensor", axis=0, tiled=True)
+    ways, here, step = (lax.axis_size("tensor"), lax.axis_index("tensor"), normed_low.shape[0])
+    dims = [n * ways if d == 0 else n for d, n in enumerate(normed_low.shape)]
+    gathered = lax.dynamic_update_slice_in_dim(
+        jnp.zeros(dims, normed_low.dtype), normed_low, here * step, axis=0
+    )
+    going_up = going_down = normed_low
+    for far in range(1, ways // 2 + 1):
+        going_up = lax.ppermute(going_up, "tensor", [(d, (d + 1) % ways) for d in range(ways)])
+        gathered = lax.dynamic_update_slice_in_dim(
+            gathered, going_up, (here - far) % ways * step, axis=0
+        )
+        if 2 * far < ways:
+            going_down = lax.ppermute(
+                going_down, "tensor", [(d, (d - 1) % ways) for d in range(ways)]
+            )
+            gathered = lax.dynamic_update_slice_in_dim(
+                gathered, going_down, (here + far) % ways * step, axis=0
+            )
     group_rows = gathered.shape[0]
     num_blocks = group_rows // BLK
     seq_blocks = min(4, num_blocks // 2)

time: 760 us -> 786 us (1.034)
  waiting for transfers between devices: 378 us -> 389 us
  starting transfers between devices: 0.96 us -> 10.4 us
  local copies, waits for them, and re-layouts: 53.6 us -> 61.8 us
    ppermute x0 -> x3, waiting for transfers between devices: none -> 38 us  [the longest x2 38 us: shards(): lax.ppermute(going_up, 'tensor', [(d, (d + 1) % ways) for d in range(ways)])]
    all_gather x1 -> x0, waiting for transfers between devices: 29.4 us -> none  [shards(): gathered = lax.all_gather(normed_low, 'tensor', axis=0, tiled=True)]
    ppermute x0 -> x3, starting transfers between devices: none -> 9.51 us  [the longest x2 7.59 us: shards(): lax.ppermute(going_up, 'tensor', [(d, (d + 1) % ways) for d in range(ways)])]
  transfers between devices with their start and end apart: 8 -> 10, of which waited for: 6 -> 7; matrix products, arithmetic and copies ran while one was open for 21% -> 21% of each run, Pallas kernels for 0% -> 0%
where the time goes in v1:
time: 786 us; the launch traced here: 781 us
  waiting for transfers between devices  389 us (49%)
  matrix products  185 us (24%)
  other arithmetic  67.8 us (9%)
  local copies, waits for them, and re-layouts  61.8 us (8%)
  blocking collectives  40.9 us (5%)
  between operations  14.9 us (2%)
  loops' own time  10.9 us (1%)
  starting transfers between devices  10.4 us (1%)
    reduce_scatter x1, waiting for transfers between devices, shards(): lax.psum_scatter(grad_w_down, 'dp', scatter_dimension=1, tiled=True)  92.6 us
    reduce_scatter x1, waiting for transfers between devices, shards(): lax.psum_scatter(grad_w_in_local, 'dp', scatter_dimension=0, tiled=True)  91.5 us
    reduce_scatter x1, waiting for transfers between devices, shards(): lax.psum_scatter(grad_w_qkv_local, 'dp', scatter_dimension=1, tiled=True)  77.9 us
    reduce_scatter x1, waiting for transfers between devices, shards(): lax.psum_scatter(jnp.dot(attended, w_out_flat, preferred_element_type=jnp...  66.7 us
    psum x1, blocking collectives, shards(): lax.psum((grad_gain_part, grad_bias_part, grad_bout_part, bqkv_full, bin_...  40.9 us
    ppermute x2, waiting for transfers between devices, shards(): lax.ppermute(going_up, 'tensor', [(d, (d + 1) % ways) for d in range(ways)])  38 us
    dot_general x1, matrix products, shards(): jnp.einsum('td,fd->tf', cotangent_group, w_down, preferred_element_type=j...  26.8 us
    reduce_scatter x1, waiting for transfers between devices, shards(): lax.psum_scatter(grad_w_out.reshape(heads_local, head_dim, model_width),...  22.6 us
  transfers between devices with their start and end apart: 10, of which 7 were waited for; matrix products, arithmetic and copies ran while one was open for 21% of the time, Pallas kernels for 0%

profile of v1, /device:TPU:0, one launch (start us, length us, event | category | flops | bytes accessed | tf_op | source)
XLA Modules:
  0.0 781.5 jit_solution(5258973032276454416)
XLA Ops:
  24.6 23.1 %collective-permute-done = bf16[512,1024]{1,0:T(8,128)(2,1)} collective-permute-done((bf16[512,1024]{1,0:T(8,128)(2,1)}, bf16[512,1024]{1,0:T(8,128)(2,1)}, u32[]{:S(2)}, u32[]{:S(2)}) %collective-permute-start) | collective-permute-done | bytes 1048608 | tf_op jit(solution)/shard_map/ppermute | solution.py:60
  47.7 7.1 collective-permute-start.2
  60.3 14.9 %collective-permute-done.2 = bf16[512,1024]{1,0:T(8,128)(2,1)S(1)} collective-permute-done((bf16[512,1024]{1,0:T(8,128)(2,1)}, bf16[512,1024]{1,0:T(8,128)(2,1)S(1)}, u32[]{:S(2)}, u32[]{:S(2)}) %collective-permute-start.2) | collective-permute-done | bytes 1048608 | tf_op jit(solution)/shard_map/ppermute | solution.py:60
  76.3 13.9 %convolution_add_fusion = f32[2048,1792]{0,1:T(8,128)} fusion(bf16[2048,1024]{1,0:T(8,128)(2,1)} %constant_dynamic-update-slice_fusion.1, f32[1792]{0:T(1024)S(1)} %pad_maximum_fusion.8, bf16[1024,1024]{1,0:T(8,128)(2,1)S(1)} %copy-done.38, bf16[1024,256]{1,0:T(8,128)(2,1)S(1)} %copy-done.22, bf16[1024,256]{1,0:T(8,128)(2,1)S(1)} %copy-done.20, ...), kind=kOutput, calls=%fused_computation.77 | convolution fusion | flops 7534542848 | bytes 22551552 | tf_op jit(solution)/shard_map/dot_general | solution.py:86
  98.4 59.7 %while.31 = (s32[]{:T(128)}, bf16[4,512,4,64]{1,3,2,0:T(8,128)(2,1)}, f32[4,4,512]{2,1,0:T(4,128)}, s32[4]{0:T(128)S(1)}, bf16[2560,4,64]{0,2,1:T(8,128)(2,1)}, ...) while((s32[]{:T(128)}, ...), condition=%wide.region_6.7_spmd.clone, body=%wide.region_3.6_spmd.clone.sunk | while | flops 563084288 | bytes 29175080 | solution.py:134
  167.8 80.2 %while.32 = (s32[]{:T(128)}, f32[2048,4,64]{0,2,1:T(8,128)}, f32[2560,4,64]{0,2,1:T(8,128)}, f32[2560,4,64]{0,2,1:T(8,128)}, bf16[2560,4,64]{0,2,1:T(8,128)(2,1)...) while((s32[]{:T(128)}, f32[2048,4,64]{0,2,1:T(8,128)}, ...), condition=%wide.region_10.11_spmd.clone, body=%wide.region_8.10_spmd.clone.sunk | while | flops 1375599616 | bytes 97585616 | solution.py:204
  183.5 4.5 fusion.144
  223.5 4.5 fusion.144
  243.5 4.5 fusion.144
  254.6 26.8 %add_convert_fusion = (bf16[2048,1024]{0,1:T(8,128)(2,1)S(1)}, f32[2048,1024]{0,1:T(8,128)}) fusion(f32[2048,1792]{0,1:T(8,128)} %convolution_add_fusion, bf16[2048,1024]{1,0:T(8,128)(2,1)S(1)} %copy-done.37, bf16[1024,1024]{1,0:T(8,128)(2,1)S(1)} %copy-done), kind=kOutput, calls=%fused_computation.61 | convolution fusion | flops 4445962240 | bytes 27262976 | tf_op jit(solution)/shard_map/td,fd->tf/dot_general | solution.py:154
  283.3 12.7 %fusion.79 = f32[2048,1024]{1,0:T(8,128)} fusion(bf16[1024,1024]{1,0:T(8,128)(2,1)} %param.21, bf16[1024,256]{1,0:T(8,128)(2,1)S(1)} %copy-done.23, bf16[1024,256]{1,0:T(8,128)(2,1)S(1)} %copy-done.21, bf16[1024,256]{1,0:T(8,128)(2,1)S(1)} %copy-done.19, bf16[2048,1024]{0,1:T(8,128)(2,1)S(1)} %get-tuple-element.373, bf16[2048,256]{0,1:T(8,128)(2,1)S(1)} %bitcast.104, ...), kind=kOutput, calls=%fused_computation.119 | convolution fusion | flops 7560232960 | bytes 19398656 | tf_op jit(solution)/shard_map/tc,dc->td/dot_general | solution.py:226
  298.6 11.4 %multiply_convert_fusion.1 = bf16[2048,1024]{0,1:T(8,128)(2,1)} fusion(f32[2048,1024]{0,1:T(8,128)} %get-tuple-element.374, f32[2048,1792]{0,1:T(8,128)} %convolution_add_fusion), kind=kLoop, calls=%fused_computation.62 | loop fusion | flops 6291456 | bytes 20971520 | tf_op jit(solution)/shard_map/convert_element_type | solution.py:138
  310.0 7.0 fusion.92
  317.0 4.8 convolution_add_fusion.1
  326.6 12.1 %fusion.85 = f32[1024,1792]{1,0:T(8,128)S(1)} fusion(bf16[2048,1024]{1,0:T(8,128)(2,1)} %constant_dynamic-update-slice_fusion.1, bf16[2048,1024]{0,1:T(8,128)(2,1)} %copy-done.8, bf16[2048,256]{0,1:T(8,128)(2,1)} %bitcast.105, bf16[2048,256]{0,1:T(8,128)(2,1)} %bitcast.114, bf16[2048,256]{0,1:T(8,128)(2,1)} %bitcast.111), kind=kOutput, calls=%fused_computation.153 | convolution fusion | flops 7545552896 | bytes 18874368 | tf_op jit(solution)/shard_map/td,tc->dc/dot_general | solution.py:221
  354.0 4.8 slice.139
  359.1 10.0 %fusion.93 = f32[1024,1024]{1,0:T(8,128)} fusion(bf16[2048,1024]{0,1:T(8,128)(2,1)} %multiply_convert_fusion.1, bf16[2048,1024]{1,0:T(8,128)(2,1)} %all-gather.2.cloned.1.call-done), kind=kOutput, calls=%fused_computation.159 | convolution fusion | flops 4294967296 | bytes 12582912 | tf_op jit(solution)/shard_map/tf,td->fd/dot_general | solution.py:160
  377.0 66.7 %reduce-scatter.7.cloned.1.call-done = f32[512,1024]{1,0:T(8,128)} async-done(((f32[2048,1024]{1,0:T(8,128)}), f32[512,1024]{1,0:T(8,128)}) %reduce-scatter.7.cloned.1.call-update) | async-done | bytes 2097168 | tf_op jit(solution)/shard_map/reduce_scatter | solution.py:142
  443.7 5.1 convert_reduce_fusion.2
  448.9 40.9 %all-reduce.2 = (f32[1024]{0:T(1024)}, f32[1024]{0:T(1024)}, f32[3,16,64]{2,1,0:T(8,128)}, f32[4096]{0:T(1024)}, f32[1024]{0:T(1024)}) all-reduce(f32[1024]{0:T(1024)S(1)} %get-tuple-element.320, f32[1024]{0:T(1024)S(1)} %get-tuple-element.322, ...), channel_id=1, replica_groups=mesh['dp'=8,'tensor'=4] {'dp','tensor'}, use_global_device_ids=true, to_apply=%region_15.16 | all-reduce | flops 10240 | bytes 81920 | tf_op jit(solution)/shard_map/psum | solution.py:254
  489.8 22.6 %reduce-scatter.15.cloned.1.call-done = f32[4,64,128]{2,1,0:T(8,128)} async-done(((f32[4,64,1024]{2,1,0:T(8,128)}), f32[4,64,128]{2,1,0:T(8,128)}) %reduce-scatter.15.cloned.1.call-update) | async-done | bytes 131088 | tf_op jit(solution)/shard_map/reduce_scatter | solution.py:260
  512.4 77.9 %reduce-scatter.11.cloned.1.call-done = f32[3,128,4,64]{1,3,2,0:T(8,128)} async-done(((f32[3,1024,4,64]{1,3,2,0:T(8,128)}), f32[3,128,4,64]{1,3,2,0:T(8,128)}) %reduce-scatter.11.cloned.1.call-update) | async-done | bytes 393232 | tf_op jit(solution)/shard_map/reduce_scatter | solution.py:258
  590.3 91.5 %reduce-scatter.13.cloned.1.call-done = f32[128,1024]{1,0:T(8,128)} async-done(((f32[1024,1024]{1,0:T(8,128)}), f32[128,1024]{1,0:T(8,128)}) %reduce-scatter.13.cloned.1.call-update) | async-done | bytes 524304 | tf_op jit(solution)/shard_map/reduce_scatter | solution.py:259
  681.8 92.6 %reduce-scatter.17.cloned.1.call-done = f32[1024,128]{1,0:T(8,128)} async-done(((f32[1024,1024]{1,0:T(8,128)}), f32[1024,128]{1,0:T(8,128)}) %reduce-scatter.17.cloned.1.call-update) | async-done | bytes 524304 | tf_op jit(solution)/shard_map/reduce_scatter | solution.py:266
  (259 shorter events, 196.2 us)
Async XLA Ops:
  7.2 247.3 %copy-start = (bf16[1024,1024]{1,0:T(8,128)(2,1)S(1)}, bf16[1024,1024]{1,0:T(8,128)(2,1)}, u32[]{:S(2)}) copy-start(bf16[1024,1024]{1,0:T(8,128)(2,1)} %param.24) | copy-start | bytes 6291460
  7.2 150.9 %all-gather.2.cloned.1.call-start = ((), (), s32[]{:S(2)}) async-start(), calls=%async_computation.7 | async-start | bytes 5242880 | tf_op jit(solution)/shard_map/all_gather | solution.py:150
  15.2 32.5 %collective-permute-start = (bf16[512,1024]{1,0:T(8,128)(2,1)}, bf16[512,1024]{1,0:T(8,128)(2,1)}, u32[]{:S(2)}, u32[]{:S(2)}) collective-permute-start(bf16[512,1024]{1,0:T(8,128)(2,1)} %get-tuple-element.376), channel_id=1, source_target_pairs={{0,1},{1,2},{2,3},{3,0},{4,5},{5,6},{6,7},{7,4},{8,9},{9,10},{10,1... | collective-permute-start | bytes 3145736 | tf_op jit(solution)/shard_map/ppermute | solution.py:60
  15.7 42.4 %collective-permute-start.1 = (bf16[512,1024]{1,0:T(8,128)(2,1)}, bf16[512,1024]{1,0:T(8,128)(2,1)}, u32[]{:S(2)}, u32[]{:S(2)}) collective-permute-start(bf16[512,1024]{1,0:T(8,128)(2,1)} %get-tuple-element.376), channel_id=1, source_target_pairs={{0,3},{1,0},{2,1},{3,2},{4,7},{5,4},{6,5},{7,6},{8,11},{9,8},{10,9... | collective-permute-start | bytes 3145736 | tf_op jit(solution)/shard_map/ppermute | solution.py:65
  17.6 356.0 %reduce-scatter.9.cloned.1.call-start = ((), (), s32[]{:S(2)}) async-start(), calls=%async_computation.8 | async-start | bytes 10485760 | tf_op jit(solution)/shard_map/reduce_scatter | solution.py:225
  23.4 52.9 %copy-start.18 = (bf16[1024,256]{1,0:T(8,128)(2,1)S(1)}, bf16[1024,256]{1,0:T(8,128)(2,1)}, u32[]{:S(2)}) copy-start(bf16[1024,256]{1,0:T(8,128)(2,1)} %copy.36) | copy-start | bytes 1572868
  24.4 51.9 %copy-start.20 = (bf16[1024,256]{1,0:T(8,128)(2,1)S(1)}, bf16[1024,256]{1,0:T(8,128)(2,1)}, u32[]{:S(2)}) copy-start(bf16[1024,256]{1,0:T(8,128)(2,1)} %copy.37) | copy-start | bytes 1572868
  24.6 51.7 %copy-start.22 = (bf16[1024,256]{1,0:T(8,128)(2,1)S(1)}, bf16[1024,256]{1,0:T(8,128)(2,1)}, u32[]{:S(2)}) copy-start(bf16[1024,256]{1,0:T(8,128)(2,1)} %copy.38) | copy-start | bytes 1572868
  24.6 51.7 %copy-start.38 = (bf16[1024,1024]{1,0:T(8,128)(2,1)S(1)}, bf16[1024,1024]{1,0:T(8,128)(2,1)}, u32[]{:S(2)}) copy-start(bf16[1024,1024]{1,0:T(8,128)(2,1)} %param.21) | copy-start | bytes 6291460
  47.7 27.5 %collective-permute-start.2 = (bf16[512,1024]{1,0:T(8,128)(2,1)}, bf16[512,1024]{1,0:T(8,128)(2,1)S(1)}, u32[]{:S(2)}, u32[]{:S(2)}) collective-permute-start(bf16[512,1024]{1,0:T(8,128)(2,1)} %collective-permute-done), channel_id=1, source_target_pairs={{0,1},{1,2},{2,3},{3,0},{4,5},{5,6},{6,7},{7,4},{8,9},{9,10},{10,1... | collective-permute-start | bytes 3145736 | tf_op jit(solution)/shard_map/ppermute | solution.py:60
  55.8 40.2 %copy-start.14 = (f32[2048,8]{0,1:T(8,128)}, f32[2048,8]{0,1:T(8,128)S(1)}, u32[]{:S(2)}) copy-start(f32[2048,8]{0,1:T(8,128)S(1)} %get-tuple-element.406) | copy-start | bytes 196612
  98.4 59.7 %copy-start.16 = (bf16[4,64,1024]{2,1,0:T(8,128)(2,1)S(1)}, bf16[4,64,1024]{2,1,0:T(8,128)(2,1)}, u32[]{:S(2)}) copy-start(bf16[4,64,1024]{2,1,0:T(8,128)(2,1)} %param.23) | copy-start | bytes 1572868
  167.8 83.2 %copy-start.15 = (f32[2048,8]{0,1:T(8,128)S(1)}, f32[2048,8]{0,1:T(8,128)}, u32[]{:S(2)}) copy-start(f32[2048,8]{0,1:T(8,128)} %copy-done.14) | copy-start | bytes 196612
  167.8 83.3 %copy-start.24 = (f32[2048,8]{0,1:T(8,128)S(1)}, f32[2048,8]{0,1:T(8,128)}, u32[]{:S(2)}) copy-start(f32[2048,8]{0,1:T(8,128)} %get-tuple-element.404) | copy-start | bytes 196612
  254.3 27.0 %copy-start.10 = (bf16[2048,4,64]{0,2,1:T(8,128)(2,1)}, bf16[2048,4,64]{0,2,1:T(8,128)(2,1)S(1)}, u32[]{:S(2)}) copy-start(bf16[2048,4,64]{0,2,1:T(8,128)(2,1)S(1)} %slice.174) | copy-start | bytes 3145732
  254.5 28.8 %copy-start.19 = (bf16[1024,256]{1,0:T(8,128)(2,1)S(1)}, bf16[1024,256]{1,0:T(8,128)(2,1)}, u32[]{:S(2)}) copy-start(bf16[1024,256]{1,0:T(8,128)(2,1)} %copy.36) | copy-start | bytes 1572868
  254.6 28.8 %copy-start.21 = (bf16[1024,256]{1,0:T(8,128)(2,1)S(1)}, bf16[1024,256]{1,0:T(8,128)(2,1)}, u32[]{:S(2)}) copy-start(bf16[1024,256]{1,0:T(8,128)(2,1)} %copy.37) | copy-start | bytes 1572868
  254.6 28.8 %copy-start.23 = (bf16[1024,256]{1,0:T(8,128)(2,1)S(1)}, bf16[1024,256]{1,0:T(8,128)(2,1)}, u32[]{:S(2)}) copy-start(bf16[1024,256]{1,0:T(8,128)(2,1)} %copy.38) | copy-start | bytes 1572868
  296.1 147.6 %reduce-scatter.7.cloned.1.call-start = ((), (), s32[]{:S(2)}) async-start(), calls=%async_computation.6 | async-start | bytes 10485760 | tf_op jit(solution)/shard_map/reduce_scatter | solution.py:142
  321.8 190.5 %reduce-scatter.15.cloned.1.call-start = ((), (), s32[]{:S(2)}) async-start(), calls=%async_computation.11 | async-start | bytes 1179648 | tf_op jit(solution)/shard_map/reduce_scatter | solution.py:260
  326.3 263.9 %reduce-scatter.11.cloned.1.call-start = ((), (), s32[]{:S(2)}) async-start(), calls=%async_computation.9 | async-start | bytes 3538944 | tf_op jit(solution)/shard_map/reduce_scatter | solution.py:258
  353.9 327.9 %reduce-scatter.13.cloned.1.call-start = ((), (), s32[]{:S(2)}) async-start(), calls=%async_computation.10 | async-start | bytes 4718592 | tf_op jit(solution)/shard_map/reduce_scatter | solution.py:259
  358.8 415.6 %reduce-scatter.17.cloned.1.call-start = ((), (), s32[]{:S(2)}) async-start(), calls=%async_computation.12 | async-start | bytes 4718592 | tf_op jit(solution)/shard_map/reduce_scatter | solution.py:266
  373.5 70.2 %copy-start.35 = (f32[1024]{0:T(1024)S(1)}, f32[1024]{0:T(1024)}, u32[]{:S(2)}) copy-start(f32[1024]{0:T(1024)} %param.25) | copy-start | bytes 12292
  (39 other events, 202.8 us)
Sparse Core Ops, SparseCore 0:
  17.8 53.6 all-gather.1
  296.2 73.4 reduce-scatter.8
  372.3 71.4 reduce-scatter.6
  447.6 64.7 reduce-scatter.14
  516.4 73.8 reduce-scatter.10
  594.3 87.4 reduce-scatter.12
  686.0 88.3 reduce-scatter.16
